TPU v7x, 32 devices: a whole 2x2x4 slice. The times are simulated.
32 devices in a mesh: grp: 2 (over y), skill: 16 (over z, x, core).
Axes of the slice: x: 2, y: 2, z: 4, core: 2. Of those that a mesh axis runs over, the one named last changes fastest.
Arguments:
- value_next: bfloat16 [2048, 4, 2048], P('skill', 'grp'), parts along dimension 1, may hold values from -6 to 6
- income_matrix: float32 [64, 32], P('grp'), parts along dimension 0, may hold values from -1 to 1
- block_weights: bfloat16 [16, 16, 4, 128, 128], P('skill')
- block_offset: int32 [16, 16, 4], P('skill'), may hold values from 0 to 3, as said below
- block_count: int32 [16, 16], P('skill'), may hold values from 1 to 4, as said below
- asset_next: int32 [16, 2, 2048], replicated, may hold values from 0 to 1
- flow: float32 [32, 2, 2048], P('grp'), parts along dimension 0, may hold values from -4 to 15
Outputs:
- value_now: bfloat16 [2048, 4, 2048], P('skill', 'grp'), parts along dimension 1
There are 2 independent parts, one for each index of `grp`. A program takes and returns all parts, laid end to end along the dimension named above; an argument that names none is the same for every part. Nothing has to cross between parts.
Inputs may be any that keep to these rules, and one draw needn't show every extreme that they name: `block_offset`: each row of 4 entries is a permutation of 0 to 3, the same for every level. `block_count`: the same for every level.
All inputs are finite; a program needn't handle non-finite values.
Results may differ from a plain program's by a relative error of at most 0.0031.
Values may be sent and summed in bfloat16 or wider, within the bound.
A program may use at most 128 MiB of HBM per device.

v0:
```python
import jax
import jax.numpy as jnp
from jax import lax
from jax.sharding import PartitionSpec as P


def shifted(block, axis, distance):
    devices = range(lax.axis_size(axis))
    route = [(i - distance, i) for i in devices if i - distance in devices]
    return lax.ppermute(block, axis, route)


def on_device(
    value_next, income_matrix, block_weights, block_offset, block_count, asset_next, flow
):
    tiles = lax.axis_size("skill")
    local_rows, assets, skills = value_next.shape
    tile = skills // tiles
    rows = local_rows * tiles
    shocks = income_matrix.shape[0]
    parents = rows // shocks
    blocks = block_offset.shape[-1]
    levels = block_offset.shape[1]
    arrived = lax.all_to_all(value_next, "skill", split_axis=2, concat_axis=0, tiled=True)
    width = arrived.shape[2]
    grid = arrived.astype(jnp.float32).reshape(parents, shocks, assets * width)
    mixed = jnp.einsum("fe,hex->hfx", income_matrix, grid, precision=lax.Precision.HIGHEST)
    own_tile = mixed.reshape(rows, assets, width).astype(jnp.bfloat16)
    gathered = [own_tile]
    for step in range(1, blocks):
        gathered.append(shifted(own_tile, "skill", -step))
    window = jnp.concatenate(gathered, axis=2)
    matrix = window.reshape(rows * assets, blocks * tile)
    place = jnp.arange(blocks, dtype=jnp.int32)
    offsets = block_offset[0]
    counts = block_count[0]
    select = (
        (offsets[:, :, None] == place[None, None, :])
        & (place[None, :, None] < counts[:, None, None])
    ).astype(jnp.float32)
    transit = jnp.einsum("ikr,ikst->irts", select, block_weights[0].astype(jnp.float32))
    transit = transit.astype(jnp.bfloat16).reshape(levels, blocks * tile, tile)
    flow_rows = jnp.transpose(flow, (0, 2, 1))[..., None]
    choose = jnp.transpose(asset_next, (0, 2, 1))

    def level_step(index, carry):
        running_max, running_total = carry
        cont = jnp.dot(matrix, transit[index], preferred_element_type=jnp.float32).reshape(
            rows, assets, tile
        )
        chosen = choose[index][:, :, None]
        picked = jnp.zeros((rows, assets, tile), jnp.float32)
        for option in range(assets):
            picked = picked + jnp.where(chosen == option, cont[:, option : option + 1, :], 0.0)
        score = (flow_rows[index] + 0.96 * picked) / 0.05
        new_max = jnp.maximum(running_max, score)
        new_total = running_total * jnp.exp(running_max - new_max) + jnp.exp(score - new_max)
        return (new_max, new_total)

    start_max = jnp.full((rows, assets, tile), -jnp.inf, jnp.float32)
    start_total = jnp.zeros((rows, assets, tile), jnp.float32)
    final_max, final_total = lax.fori_loop(0, levels, level_step, (start_max, start_total))
    value_tile = (0.05 * (final_max + jnp.log(final_total))).astype(jnp.bfloat16)
    return lax.all_to_all(value_tile, "skill", split_axis=0, concat_axis=2, tiled=True)


def solution(mesh):
    placed = (
        P("skill", "grp", None),
        P("grp", None),
        P("skill", None, None, None, None),
        P("skill", None, None),
        P("skill", None),
        P(),
        P("grp", None, None),
    )
    return jax.shard_map(
        on_device, mesh=mesh, in_specs=placed, out_specs=P("skill", "grp", None), check_vma=False
    )
```

profile of v0, /device:TPU:1, one launch (start us, length us, event | category | flops | bytes accessed | tf_op | source)
XLA Modules:
  0.0 645.9 jit_solution(14439508790451273633)
XLA Ops:
  0.0 4.9 copy.39
  4.9 32.5 %all_to_all.33 = bf16[128,2,2048]{0,1,2:T(2,128)(2,1)S(1)} all-to-all(bf16[128,2,2048]{0,1,2:T(2,128)(2,1)} %copy.39), channel_id=1, replica_groups=mesh['grp'=2,'skill'=16] {'skill'}, dimensions={2} | all-to-all | bytes 2097152 | tf_op jit(solution)/shard_map/all_to_all | solution.py:24
  54.1 4.2 copy.44
  58.3 8.6 %copy.36 = s32[16,2,2048]{1,2,0:T(8,128)} copy(s32[16,2,2048]{2,1,0:T(2,128)S(1)} %copy-done.3) | data formatting | bytes 524288 | tf_op args[5]
  66.9 8.6 %copy.35 = f32[16,2,2048]{1,2,0:T(8,128)} copy(f32[16,2,2048]{2,1,0:T(2,128)S(1)} %copy-done.4) | data formatting | bytes 524288 | tf_op args[6]
  75.5 17.9 %collective-permute-done.1 = bf16[2048,2,128]{2,1,0:T(2,128)(2,1)} collective-permute-done((bf16[2048,2,128]{2,1,0:T(2,128)(2,1)S(1)}, bf16[2048,2,128]{2,1,0:T(2,128)(2,1)}, u32[]{:S(2)}, u32[]{:S(2)}) %collective-permute-start.1) | collective-permute-done | bytes 1048608 | tf_op jit(solution)/shard_map/ppermute | solution.py:10
  95.2 8.8 %pad_maximum_fusion = bf16[2048,2,512]{2,1,0:T(2,128)(2,1)} fusion(bf16[2048,2,128]{2,1,0:T(2,128)(2,1)} %collective-permute-done.2, bf16[2048,2,128]{2,1,0:T(2,128)(2,1)} %collective-permute-done.1, bf16[2048,2,128]{2,1,0:T(2,128)(2,1)} %collective-permute-done, bf16[2048,2,128]{2,1,0:T(2,128)(2,1)S(1)} %convert_element_type.25), kind=kLoop, calls=%fused_computation.12 | loop fusion | flops 16777216 | bytes 8388608 | tf_op jit(solution)/shard_map/concatenate | solution.py:32
  103.9 7.2 %reshape.73 = bf16[4096,512]{1,0:T(8,128)(2,1)} reshape(bf16[2048,2,512]{2,1,0:T(2,128)(2,1)} %pad_maximum_fusion) | data formatting | bytes 8388608 | tf_op jit(solution)/shard_map/reshape | solution.py:33
  111.1 487.8 %while.16 = (s32[]{:T(128)}, f32[2048,2,128]{2,1,0:T(2,128)}, f32[2048,2,128]{2,1,0:T(2,128)}, f32[16,2048,2,1]{2,1,3,0:T(8,128)}, s32[16,2048,2]{2,1,0:T(8,128)...) while((s32[]{:T(128)}, f32[2048,2,128]{2,1,0:T(2,128)}, ...), condition=%wide.region_1.2_spmd.clone, body=%wide.region_0.1_spmd.clone.sunk | while | flops 543694848 | bytes 25395352 | solution.py:62
  120.2 3.9 fusion.26
  124.1 16.8 %fusion.27 = (f32[2048,2,128]{2,1,0:T(2,128)}, f32[2048,2,128]{2,1,0:T(2,128)}) fusion(f32[2048,2,128]{2,1,0:T(2,128)} %get-tuple-element.270, pred[]{:T(512)S(6)} %compare.3, f32[2048,2,128]{2,1,0:T(2,128)} %get-tuple-element.269, f32[2048,128]{1,0:T(8,128)S(1)} %bitcast.63, pred[2048,2]{1,0:T(8,128)(4,1)S(1)} %copy-done.2, ...), kind=kLoop, calls=%fused_computation.2.clone.1 | loop fusion | flops 6815744 | bytes 10510337 | tf_op jit(solution)/shard_map/while/body/eval_jaxpr/add | solution.py:57
  150.1 3.9 fusion.26
  154.0 17.5 %fusion.27 = (f32[2048,2,128]{2,1,0:T(2,128)}, f32[2048,2,128]{2,1,0:T(2,128)}) fusion(f32[2048,2,128]{2,1,0:T(2,128)} %get-tuple-element.270, pred[]{:T(512)S(6)} %compare.3, f32[2048,2,128]{2,1,0:T(2,128)} %get-tuple-element.269, f32[2048,128]{1,0:T(8,128)S(1)} %bitcast.63, pred[2048,2]{1,0:T(8,128)(4,1)S(1)} %copy-done.2, ...), kind=kLoop, calls=%fused_computation.2.clone.1 | loop fusion | flops 6815744 | bytes 10510337 | tf_op jit(solution)/shard_map/while/body/eval_jaxpr/add | solution.py:57
  184.5 17.5 %fusion.27 = (f32[2048,2,128]{2,1,0:T(2,128)}, f32[2048,2,128]{2,1,0:T(2,128)}) fusion(f32[2048,2,128]{2,1,0:T(2,128)} %get-tuple-element.270, pred[]{:T(512)S(6)} %compare.3, f32[2048,2,128]{2,1,0:T(2,128)} %get-tuple-element.269, f32[2048,128]{1,0:T(8,128)S(1)} %bitcast.63, pred[2048,2]{1,0:T(8,128)(4,1)S(1)} %copy-done.2, ...), kind=kLoop, calls=%fused_computation.2.clone.1 | loop fusion | flops 6815744 | bytes 10510337 | tf_op jit(solution)/shard_map/while/body/eval_jaxpr/add | solution.py:57
  215.1 17.5 %fusion.27 = (f32[2048,2,128]{2,1,0:T(2,128)}, f32[2048,2,128]{2,1,0:T(2,128)}) fusion(f32[2048,2,128]{2,1,0:T(2,128)} %get-tuple-element.270, pred[]{:T(512)S(6)} %compare.3, f32[2048,2,128]{2,1,0:T(2,128)} %get-tuple-element.269, f32[2048,128]{1,0:T(8,128)S(1)} %bitcast.63, pred[2048,2]{1,0:T(8,128)(4,1)S(1)} %copy-done.2, ...), kind=kLoop, calls=%fused_computation.2.clone.1 | loop fusion | flops 6815744 | bytes 10510337 | tf_op jit(solution)/shard_map/while/body/eval_jaxpr/add | solution.py:57
  241.7 3.9 fusion.26
  245.6 17.5 %fusion.27 = (f32[2048,2,128]{2,1,0:T(2,128)}, f32[2048,2,128]{2,1,0:T(2,128)}) fusion(f32[2048,2,128]{2,1,0:T(2,128)} %get-tuple-element.270, pred[]{:T(512)S(6)} %compare.3, f32[2048,2,128]{2,1,0:T(2,128)} %get-tuple-element.269, f32[2048,128]{1,0:T(8,128)S(1)} %bitcast.63, pred[2048,2]{1,0:T(8,128)(4,1)S(1)} %copy-done.2, ...), kind=kLoop, calls=%fused_computation.2.clone.1 | loop fusion | flops 6815744 | bytes 10510337 | tf_op jit(solution)/shard_map/while/body/eval_jaxpr/add | solution.py:57
  272.2 3.9 fusion.26
  276.1 17.5 %fusion.27 = (f32[2048,2,128]{2,1,0:T(2,128)}, f32[2048,2,128]{2,1,0:T(2,128)}) fusion(f32[2048,2,128]{2,1,0:T(2,128)} %get-tuple-element.270, pred[]{:T(512)S(6)} %compare.3, f32[2048,2,128]{2,1,0:T(2,128)} %get-tuple-element.269, f32[2048,128]{1,0:T(8,128)S(1)} %bitcast.63, pred[2048,2]{1,0:T(8,128)(4,1)S(1)} %copy-done.2, ...), kind=kLoop, calls=%fused_computation.2.clone.1 | loop fusion | flops 6815744 | bytes 10510337 | tf_op jit(solution)/shard_map/while/body/eval_jaxpr/add | solution.py:57
  302.7 3.9 fusion.26
  306.7 17.5 %fusion.27 = (f32[2048,2,128]{2,1,0:T(2,128)}, f32[2048,2,128]{2,1,0:T(2,128)}) fusion(f32[2048,2,128]{2,1,0:T(2,128)} %get-tuple-element.270, pred[]{:T(512)S(6)} %compare.3, f32[2048,2,128]{2,1,0:T(2,128)} %get-tuple-element.269, f32[2048,128]{1,0:T(8,128)S(1)} %bitcast.63, pred[2048,2]{1,0:T(8,128)(4,1)S(1)} %copy-done.2, ...), kind=kLoop, calls=%fused_computation.2.clone.1 | loop fusion | flops 6815744 | bytes 10510337 | tf_op jit(solution)/shard_map/while/body/eval_jaxpr/add | solution.py:57
  333.3 3.9 fusion.26
  337.2 17.5 %fusion.27 = (f32[2048,2,128]{2,1,0:T(2,128)}, f32[2048,2,128]{2,1,0:T(2,128)}) fusion(f32[2048,2,128]{2,1,0:T(2,128)} %get-tuple-element.270, pred[]{:T(512)S(6)} %compare.3, f32[2048,2,128]{2,1,0:T(2,128)} %get-tuple-element.269, f32[2048,128]{1,0:T(8,128)S(1)} %bitcast.63, pred[2048,2]{1,0:T(8,128)(4,1)S(1)} %copy-done.2, ...), kind=kLoop, calls=%fused_computation.2.clone.1 | loop fusion | flops 6815744 | bytes 10510337 | tf_op jit(solution)/shard_map/while/body/eval_jaxpr/add | solution.py:57
  367.7 17.5 %fusion.27 = (f32[2048,2,128]{2,1,0:T(2,128)}, f32[2048,2,128]{2,1,0:T(2,128)}) fusion(f32[2048,2,128]{2,1,0:T(2,128)} %get-tuple-element.270, pred[]{:T(512)S(6)} %compare.3, f32[2048,2,128]{2,1,0:T(2,128)} %get-tuple-element.269, f32[2048,128]{1,0:T(8,128)S(1)} %bitcast.63, pred[2048,2]{1,0:T(8,128)(4,1)S(1)} %copy-done.2, ...), kind=kLoop, calls=%fused_computation.2.clone.1 | loop fusion | flops 6815744 | bytes 10510337 | tf_op jit(solution)/shard_map/while/body/eval_jaxpr/add | solution.py:57
  398.3 17.5 %fusion.27 = (f32[2048,2,128]{2,1,0:T(2,128)}, f32[2048,2,128]{2,1,0:T(2,128)}) fusion(f32[2048,2,128]{2,1,0:T(2,128)} %get-tuple-element.270, pred[]{:T(512)S(6)} %compare.3, f32[2048,2,128]{2,1,0:T(2,128)} %get-tuple-element.269, f32[2048,128]{1,0:T(8,128)S(1)} %bitcast.63, pred[2048,2]{1,0:T(8,128)(4,1)S(1)} %copy-done.2, ...), kind=kLoop, calls=%fused_computation.2.clone.1 | loop fusion | flops 6815744 | bytes 10510337 | tf_op jit(solution)/shard_map/while/body/eval_jaxpr/add | solution.py:57
  428.8 17.5 %fusion.27 = (f32[2048,2,128]{2,1,0:T(2,128)}, f32[2048,2,128]{2,1,0:T(2,128)}) fusion(f32[2048,2,128]{2,1,0:T(2,128)} %get-tuple-element.270, pred[]{:T(512)S(6)} %compare.3, f32[2048,2,128]{2,1,0:T(2,128)} %get-tuple-element.269, f32[2048,128]{1,0:T(8,128)S(1)} %bitcast.63, pred[2048,2]{1,0:T(8,128)(4,1)S(1)} %copy-done.2, ...), kind=kLoop, calls=%fused_computation.2.clone.1 | loop fusion | flops 6815744 | bytes 10510337 | tf_op jit(solution)/shard_map/while/body/eval_jaxpr/add | solution.py:57
  459.3 17.5 %fusion.27 = (f32[2048,2,128]{2,1,0:T(2,128)}, f32[2048,2,128]{2,1,0:T(2,128)}) fusion(f32[2048,2,128]{2,1,0:T(2,128)} %get-tuple-element.270, pred[]{:T(512)S(6)} %compare.3, f32[2048,2,128]{2,1,0:T(2,128)} %get-tuple-element.269, f32[2048,128]{1,0:T(8,128)S(1)} %bitcast.63, pred[2048,2]{1,0:T(8,128)(4,1)S(1)} %copy-done.2, ...), kind=kLoop, calls=%fused_computation.2.clone.1 | loop fusion | flops 6815744 | bytes 10510337 | tf_op jit(solution)/shard_map/while/body/eval_jaxpr/add | solution.py:57
  489.9 17.5 %fusion.27 = (f32[2048,2,128]{2,1,0:T(2,128)}, f32[2048,2,128]{2,1,0:T(2,128)}) fusion(f32[2048,2,128]{2,1,0:T(2,128)} %get-tuple-element.270, pred[]{:T(512)S(6)} %compare.3, f32[2048,2,128]{2,1,0:T(2,128)} %get-tuple-element.269, f32[2048,128]{1,0:T(8,128)S(1)} %bitcast.63, pred[2048,2]{1,0:T(8,128)(4,1)S(1)} %copy-done.2, ...), kind=kLoop, calls=%fused_computation.2.clone.1 | loop fusion | flops 6815744 | bytes 10510337 | tf_op jit(solution)/shard_map/while/body/eval_jaxpr/add | solution.py:57
  520.4 17.5 %fusion.27 = (f32[2048,2,128]{2,1,0:T(2,128)}, f32[2048,2,128]{2,1,0:T(2,128)}) fusion(f32[2048,2,128]{2,1,0:T(2,128)} %get-tuple-element.270, pred[]{:T(512)S(6)} %compare.3, f32[2048,2,128]{2,1,0:T(2,128)} %get-tuple-element.269, f32[2048,128]{1,0:T(8,128)S(1)} %bitcast.63, pred[2048,2]{1,0:T(8,128)(4,1)S(1)} %copy-done.2, ...), kind=kLoop, calls=%fused_computation.2.clone.1 | loop fusion | flops 6815744 | bytes 10510337 | tf_op jit(solution)/shard_map/while/body/eval_jaxpr/add | solution.py:57
  550.9 17.5 %fusion.27 = (f32[2048,2,128]{2,1,0:T(2,128)}, f32[2048,2,128]{2,1,0:T(2,128)}) fusion(f32[2048,2,128]{2,1,0:T(2,128)} %get-tuple-element.270, pred[]{:T(512)S(6)} %compare.3, f32[2048,2,128]{2,1,0:T(2,128)} %get-tuple-element.269, f32[2048,128]{1,0:T(8,128)S(1)} %bitcast.63, pred[2048,2]{1,0:T(8,128)(4,1)S(1)} %copy-done.2, ...), kind=kLoop, calls=%fused_computation.2.clone.1 | loop fusion | flops 6815744 | bytes 10510337 | tf_op jit(solution)/shard_map/while/body/eval_jaxpr/add | solution.py:57
  581.5 17.5 %fusion.27 = (f32[2048,2,128]{2,1,0:T(2,128)}, f32[2048,2,128]{2,1,0:T(2,128)}) fusion(f32[2048,2,128]{2,1,0:T(2,128)} %get-tuple-element.270, pred[]{:T(512)S(6)} %compare.3, f32[2048,2,128]{2,1,0:T(2,128)} %get-tuple-element.269, f32[2048,128]{1,0:T(8,128)S(1)} %bitcast.63, pred[2048,2]{1,0:T(8,128)(4,1)S(1)} %copy-done.2, ...), kind=kLoop, calls=%fused_computation.2.clone.1 | loop fusion | flops 6815744 | bytes 10510337 | tf_op jit(solution)/shard_map/while/body/eval_jaxpr/add | solution.py:57
  602.4 41.1 %all_to_all.34 = bf16[2048,2,128]{2,1,0:T(2,128)(2,1)S(1)} all-to-all(bf16[2048,2,128]{2,1,0:T(2,128)(2,1)S(1)} %multiply_convert_fusion), channel_id=1, replica_groups=mesh['grp'=2,'skill'=16] {'skill'}, dimensions={0} | all-to-all | bytes 2097152 | tf_op jit(solution)/shard_map/all_to_all | solution.py:64
  (137 shorter events, 208.4 us)
Async XLA Ops:
  0.0 51.0 %copy-start = (bf16[1,16,4,128,128]{4,3,2,1,0:T(8,128)(2,1)S(1)}, bf16[1,16,4,128,128]{4,3,2,1,0:T(8,128)(2,1)}, u32[]{:S(2)}) copy-start(bf16[1,16,4,128,128]{4,3,2,1,0:T(8,128)(2,1)} %param.11) | copy-start | bytes 6291460
  37.5 5.5 copy-start.5
  43.0 7.9 %copy-start.6 = (s32[1,16,4]{1,2,0:T(4,128)S(1)}, s32[1,16,4]{1,2,0:T(4,128)}, u32[]{:S(2)}) copy-start(s32[1,16,4]{1,2,0:T(4,128)} %param.12) | copy-start | bytes 772
  43.0 7.9 %copy-start.7 = (s32[1,16]{1,0:T(1,128)S(1)}, s32[1,16]{1,0:T(1,128)}, u32[]{:S(2)}) copy-start(s32[1,16]{1,0:T(1,128)} %param.13) | copy-start | bytes 196
  46.3 29.2 %collective-permute-start.2 = (bf16[2048,2,128]{2,1,0:T(2,128)(2,1)S(1)}, bf16[2048,2,128]{2,1,0:T(2,128)(2,1)}, u32[]{:S(2)}, u32[]{:S(2)}) collective-permute-start(bf16[2048,2,128]{2,1,0:T(2,128)(2,1)S(1)} %convert_element_type.25), channel_id=1, source_target_pairs={{3,0},{4,1},{5,2},{6,3},{7,4},{8,5},{9,6},{10,7},{11,8},{12,9},{13... | collective-permute-start | bytes 3145736 | tf_op jit(solution)/shard_map/ppermute | solution.py:10
  47.6 45.8 %collective-permute-start.1 = (bf16[2048,2,128]{2,1,0:T(2,128)(2,1)S(1)}, bf16[2048,2,128]{2,1,0:T(2,128)(2,1)}, u32[]{:S(2)}, u32[]{:S(2)}) collective-permute-start(bf16[2048,2,128]{2,1,0:T(2,128)(2,1)S(1)} %convert_element_type.25), channel_id=1, source_target_pairs={{2,0},{3,1},{4,2},{5,3},{6,4},{7,5},{8,6},{9,7},{10,8},{11,9},{12,... | collective-permute-start | bytes 3145736 | tf_op jit(solution)/shard_map/ppermute | solution.py:10
  48.9 46.3 %collective-permute-start = (bf16[2048,2,128]{2,1,0:T(2,128)(2,1)S(1)}, bf16[2048,2,128]{2,1,0:T(2,128)(2,1)}, u32[]{:S(2)}, u32[]{:S(2)}) collective-permute-start(bf16[2048,2,128]{2,1,0:T(2,128)(2,1)S(1)} %convert_element_type.25), channel_id=1, source_target_pairs={{1,0},{2,1},{3,2},{4,3},{5,4},{6,5},{7,6},{8,7},{9,8},{10,9},{11,1... | collective-permute-start | bytes 3145736 | tf_op jit(solution)/shard_map/ppermute | solution.py:10
  54.1 4.2 copy-start.3
  58.3 8.6 %copy-start.4 = (f32[16,2,2048]{2,1,0:T(2,128)S(1)}, f32[16,2,2048]{2,1,0:T(2,128)}, u32[]{:S(2)}) copy-start(f32[16,2,2048]{2,1,0:T(2,128)} %param.15) | copy-start | bytes 786436
  120.2 3.9 copy-start.2
  150.0 3.9 copy-start.2
  180.6 3.9 copy-start.2
  211.1 3.9 copy-start.2
  241.7 3.9 copy-start.2
  272.2 3.9 copy-start.2
  302.7 3.9 copy-start.2
  333.3 3.9 copy-start.2
  363.8 3.9 copy-start.2
  394.3 3.9 copy-start.2
  424.9 3.9 copy-start.2
  455.4 3.9 copy-start.2
  485.9 3.9 copy-start.2
  516.5 3.9 copy-start.2
  547.0 3.9 copy-start.2
  577.5 3.9 copy-start.2
  643.5 2.3 copy-start.1
where the time goes:
time: 649 us; the launch traced here: 646 us
  other arithmetic  327 us (50%)
  local copies, waits for them, and re-layouts  155 us (24%)
  blocking collectives  73.7 us (11%)
  matrix products  65.2 us (10%)
  waiting for transfers between devices  19.7 us (3%)
    add x16, other arithmetic, level_step(): running_total * jnp.exp(running_max - new_max) + jnp.exp(score - new_max)  279 us
    slice x16, local copies, waits for them, and re-layouts, level_step(): cont[:, option:option + 1, :]  62.9 us
    dot_general x16, matrix products, level_step(): jnp.dot(matrix, transit[index], preferred_element_type=jnp.float32)  60.2 us
    all_to_all x1, blocking collectives, on_device(): lax.all_to_all(value_tile, 'skill', split_axis=0, concat_axis=2, tiled=True)  41.1 us
    eq x16, other arithmetic, level_step(): chosen == option  35.3 us
    all_to_all x1, blocking collectives, on_device(): lax.all_to_all(value_next, 'skill', split_axis=2, concat_axis=0, tiled=True)  32.5 us
    dot_general x16, local copies, waits for them, and re-layouts, level_step(): jnp.dot(matrix, transit[index], preferred_element_type=jnp.float32)  28.9 us
    unnamed x18, local copies, waits for them, and re-layouts  26.4 us
  transfers between devices with their start and end apart: 3, of which 2 were waited for; matrix products, arithmetic and copies ran while one was open for 4% of the time, Pallas kernels for 0%

commit v1 on v0

--- a/solution.py
+++ b/solution.py
@@ -21,7 +21,13 @@
     parents = rows // shocks
     blocks = block_offset.shape[-1]
     levels = block_offset.shape[1]
-    arrived = lax.all_to_all(value_next, "skill", split_axis=2, concat_axis=0, tiled=True)
+    piece_now = lax.all_to_all(
+        jnp.stack(jnp.split(value_next, lax.axis_size("skill"), axis=2), axis=0),
+        axis_name="skill",
+        concat_axis=0,
+        split_axis=0,
+    )
+    arrived = jnp.concatenate(piece_now, axis=0)
     width = arrived.shape[2]
     grid = arrived.astype(jnp.float32).reshape(parents, shocks, assets * width)
     mixed = jnp.einsum("fe,hex->hfx", income_matrix, grid, precision=lax.Precision.HIGHEST)

time: 649 us -> 654 us (level)
    unnamed x18 -> x34, local copies, waits for them, and re-layouts: 26.4 us -> 35.1 us
where the time goes in v1:
time: 654 us; the launch traced here: 651 us
  other arithmetic  326 us (50%)
  local copies, waits for them, and re-layouts  160 us (24%)
  blocking collectives  73.5 us (11%)
  matrix products  65.5 us (10%)
  waiting for transfers between devices  19.9 us (3%)
    add x16, other arithmetic, level_step(): running_total * jnp.exp(running_max - new_max) + jnp.exp(score - new_max)  279 us
    slice x16, local copies, waits for them, and re-layouts, level_step(): cont[:, option:option + 1, :]  62.2 us
    dot_general x16, matrix products, level_step(): jnp.dot(matrix, transit[index], preferred_element_type=jnp.float32)  60.3 us
    all_to_all x1, blocking collectives, on_device(): lax.all_to_all(value_tile, 'skill', split_axis=0, concat_axis=2, tiled=True)  41.1 us
    eq x16, other arithmetic, level_step(): chosen == option  35.3 us
    unnamed x34, local copies, waits for them, and re-layouts  35.1 us
    all_to_all x1, blocking collectives, on_device(): lax.all_to_all(jnp.stack(jnp.split(value_next, lax.axis_size('skill'), ax...  32.3 us
    dot_general x16, local copies, waits for them, and re-layouts, level_step(): jnp.dot(matrix, transit[index], preferred_element_type=jnp.float32)  29.1 us
  transfers between devices with their start and end apart: 3, of which 2 were waited for; matrix products, arithmetic and copies ran while one was open for 4% of the time, Pallas kernels for 0%

profile of v1, /device:TPU:1, one launch (start us, length us, event | category | flops | bytes accessed | tf_op | source)
XLA Modules:
  0.0 650.9 jit_solution(2229547621466272355)
XLA Ops:
  14.6 32.3 %all_to_all.23 = bf16[16,128,2,128]{3,2,1,0:T(2,128)(2,1)S(1)} all-to-all(bf16[16,128,2,128]{3,2,1,0:T(2,128)(2,1)S(1)} %bitcast_dynamic-update-slice_fusion), channel_id=1, replica_groups=mesh['grp'=2,'skill'=16] {'skill'}, dimensions={0} | all-to-all | bytes 2097152 | tf_op jit(solution)/shard_map/all_to_all | solution.py:24
  59.5 4.2 copy.24
  63.7 8.6 %copy.18 = s32[16,2,2048]{1,2,0:T(8,128)} copy(s32[16,2,2048]{2,1,0:T(2,128)S(1)} %copy-done.4) | data formatting | bytes 524288 | tf_op args[5]
  72.3 8.6 %copy.17 = f32[16,2,2048]{1,2,0:T(8,128)} copy(f32[16,2,2048]{2,1,0:T(2,128)S(1)} %copy-done.5) | data formatting | bytes 524288 | tf_op args[6]
  80.9 18.1 %collective-permute-done.1 = bf16[2048,2,128]{2,1,0:T(2,128)(2,1)} collective-permute-done((bf16[2048,2,128]{2,1,0:T(2,128)(2,1)}, bf16[2048,2,128]{2,1,0:T(2,128)(2,1)}, u32[]{:S(2)}, u32[]{:S(2)}) %collective-permute-start.1) | collective-permute-done | bytes 1048608 | tf_op jit(solution)/shard_map/ppermute | solution.py:10
  100.8 8.5 %pad_maximum_fusion = bf16[2048,2,512]{2,1,0:T(2,128)(2,1)} fusion(bf16[2048,2,128]{2,1,0:T(2,128)(2,1)S(1)} %collective-permute-done.2, bf16[2048,2,128]{2,1,0:T(2,128)(2,1)} %collective-permute-done.1, bf16[2048,2,128]{2,1,0:T(2,128)(2,1)} %collective-permute-done, bf16[2048,2,128]{2,1,0:T(2,128)(2,1)S(1)} %copy-done.3), kind=kLoop, calls=%fused_computation.12 | loop fusion | flops 16777216 | bytes 8388608 | tf_op jit(solution)/shard_map/concatenate | solution.py:38
  109.4 7.2 %reshape.74 = bf16[4096,512]{1,0:T(8,128)(2,1)} reshape(bf16[2048,2,512]{2,1,0:T(2,128)(2,1)} %pad_maximum_fusion) | data formatting | bytes 8388608 | tf_op jit(solution)/shard_map/reshape | solution.py:39
  116.6 487.4 %while.16 = (s32[]{:T(128)}, f32[2048,2,128]{2,1,0:T(2,128)}, f32[2048,2,128]{2,1,0:T(2,128)}, f32[16,2048,2,1]{2,1,3,0:T(8,128)}, s32[16,2048,2]{2,1,0:T(8,128)...) while((s32[]{:T(128)}, f32[2048,2,128]{2,1,0:T(2,128)}, ...), condition=%wide.region_1.2_spmd.clone, body=%wide.region_0.1_spmd.clone.sunk | while | flops 543694848 | bytes 25395352 | solution.py:68
  125.6 3.9 fusion.26
  129.5 16.8 %fusion.27 = (f32[2048,2,128]{2,1,0:T(2,128)}, f32[2048,2,128]{2,1,0:T(2,128)}) fusion(f32[2048,2,128]{2,1,0:T(2,128)} %get-tuple-element.256, pred[]{:T(512)S(6)} %compare.3, f32[2048,2,128]{2,1,0:T(2,128)} %get-tuple-element.255, f32[2048,128]{1,0:T(8,128)S(1)} %bitcast.93, pred[2048,2]{1,0:T(8,128)(4,1)S(1)} %copy-done.2, ...), kind=kLoop, calls=%fused_computation.2.clone.1 | loop fusion | flops 6815744 | bytes 10510337 | tf_op jit(solution)/shard_map/while/body/eval_jaxpr/add | solution.py:63
  155.5 3.9 fusion.26
  159.4 17.5 %fusion.27 = (f32[2048,2,128]{2,1,0:T(2,128)}, f32[2048,2,128]{2,1,0:T(2,128)}) fusion(f32[2048,2,128]{2,1,0:T(2,128)} %get-tuple-element.256, pred[]{:T(512)S(6)} %compare.3, f32[2048,2,128]{2,1,0:T(2,128)} %get-tuple-element.255, f32[2048,128]{1,0:T(8,128)S(1)} %bitcast.93, pred[2048,2]{1,0:T(8,128)(4,1)S(1)} %copy-done.2, ...), kind=kLoop, calls=%fused_computation.2.clone.1 | loop fusion | flops 6815744 | bytes 10510337 | tf_op jit(solution)/shard_map/while/body/eval_jaxpr/add | solution.py:63
  186.0 3.9 fusion.26
  189.9 17.5 %fusion.27 = (f32[2048,2,128]{2,1,0:T(2,128)}, f32[2048,2,128]{2,1,0:T(2,128)}) fusion(f32[2048,2,128]{2,1,0:T(2,128)} %get-tuple-element.256, pred[]{:T(512)S(6)} %compare.3, f32[2048,2,128]{2,1,0:T(2,128)} %get-tuple-element.255, f32[2048,128]{1,0:T(8,128)S(1)} %bitcast.93, pred[2048,2]{1,0:T(8,128)(4,1)S(1)} %copy-done.2, ...), kind=kLoop, calls=%fused_computation.2.clone.1 | loop fusion | flops 6815744 | bytes 10510337 | tf_op jit(solution)/shard_map/while/body/eval_jaxpr/add | solution.py:63
  216.5 3.9 fusion.26
  220.4 17.5 %fusion.27 = (f32[2048,2,128]{2,1,0:T(2,128)}, f32[2048,2,128]{2,1,0:T(2,128)}) fusion(f32[2048,2,128]{2,1,0:T(2,128)} %get-tuple-element.256, pred[]{:T(512)S(6)} %compare.3, f32[2048,2,128]{2,1,0:T(2,128)} %get-tuple-element.255, f32[2048,128]{1,0:T(8,128)S(1)} %bitcast.93, pred[2048,2]{1,0:T(8,128)(4,1)S(1)} %copy-done.2, ...), kind=kLoop, calls=%fused_computation.2.clone.1 | loop fusion | flops 6815744 | bytes 10510337 | tf_op jit(solution)/shard_map/while/body/eval_jaxpr/add | solution.py:63
  247.0 3.9 fusion.26
  250.9 17.5 %fusion.27 = (f32[2048,2,128]{2,1,0:T(2,128)}, f32[2048,2,128]{2,1,0:T(2,128)}) fusion(f32[2048,2,128]{2,1,0:T(2,128)} %get-tuple-element.256, pred[]{:T(512)S(6)} %compare.3, f32[2048,2,128]{2,1,0:T(2,128)} %get-tuple-element.255, f32[2048,128]{1,0:T(8,128)S(1)} %bitcast.93, pred[2048,2]{1,0:T(8,128)(4,1)S(1)} %copy-done.2, ...), kind=kLoop, calls=%fused_computation.2.clone.1 | loop fusion | flops 6815744 | bytes 10510337 | tf_op jit(solution)/shard_map/while/body/eval_jaxpr/add | solution.py:63
  277.5 3.9 fusion.26
  281.4 17.5 %fusion.27 = (f32[2048,2,128]{2,1,0:T(2,128)}, f32[2048,2,128]{2,1,0:T(2,128)}) fusion(f32[2048,2,128]{2,1,0:T(2,128)} %get-tuple-element.256, pred[]{:T(512)S(6)} %compare.3, f32[2048,2,128]{2,1,0:T(2,128)} %get-tuple-element.255, f32[2048,128]{1,0:T(8,128)S(1)} %bitcast.93, pred[2048,2]{1,0:T(8,128)(4,1)S(1)} %copy-done.2, ...), kind=kLoop, calls=%fused_computation.2.clone.1 | loop fusion | flops 6815744 | bytes 10510337 | tf_op jit(solution)/shard_map/while/body/eval_jaxpr/add | solution.py:63
  308.0 3.9 fusion.26
  311.9 17.5 %fusion.27 = (f32[2048,2,128]{2,1,0:T(2,128)}, f32[2048,2,128]{2,1,0:T(2,128)}) fusion(f32[2048,2,128]{2,1,0:T(2,128)} %get-tuple-element.256, pred[]{:T(512)S(6)} %compare.3, f32[2048,2,128]{2,1,0:T(2,128)} %get-tuple-element.255, f32[2048,128]{1,0:T(8,128)S(1)} %bitcast.93, pred[2048,2]{1,0:T(8,128)(4,1)S(1)} %copy-done.2, ...), kind=kLoop, calls=%fused_computation.2.clone.1 | loop fusion | flops 6815744 | bytes 10510337 | tf_op jit(solution)/shard_map/while/body/eval_jaxpr/add | solution.py:63
  342.4 17.5 %fusion.27 = (f32[2048,2,128]{2,1,0:T(2,128)}, f32[2048,2,128]{2,1,0:T(2,128)}) fusion(f32[2048,2,128]{2,1,0:T(2,128)} %get-tuple-element.256, pred[]{:T(512)S(6)} %compare.3, f32[2048,2,128]{2,1,0:T(2,128)} %get-tuple-element.255, f32[2048,128]{1,0:T(8,128)S(1)} %bitcast.93, pred[2048,2]{1,0:T(8,128)(4,1)S(1)} %copy-done.2, ...), kind=kLoop, calls=%fused_computation.2.clone.1 | loop fusion | flops 6815744 | bytes 10510337 | tf_op jit(solution)/shard_map/while/body/eval_jaxpr/add | solution.py:63
  372.9 17.5 %fusion.27 = (f32[2048,2,128]{2,1,0:T(2,128)}, f32[2048,2,128]{2,1,0:T(2,128)}) fusion(f32[2048,2,128]{2,1,0:T(2,128)} %get-tuple-element.256, pred[]{:T(512)S(6)} %compare.3, f32[2048,2,128]{2,1,0:T(2,128)} %get-tuple-element.255, f32[2048,128]{1,0:T(8,128)S(1)} %bitcast.93, pred[2048,2]{1,0:T(8,128)(4,1)S(1)} %copy-done.2, ...), kind=kLoop, calls=%fused_computation.2.clone.1 | loop fusion | flops 6815744 | bytes 10510337 | tf_op jit(solution)/shard_map/while/body/eval_jaxpr/add | solution.py:63
  403.4 17.5 %fusion.27 = (f32[2048,2,128]{2,1,0:T(2,128)}, f32[2048,2,128]{2,1,0:T(2,128)}) fusion(f32[2048,2,128]{2,1,0:T(2,128)} %get-tuple-element.256, pred[]{:T(512)S(6)} %compare.3, f32[2048,2,128]{2,1,0:T(2,128)} %get-tuple-element.255, f32[2048,128]{1,0:T(8,128)S(1)} %bitcast.93, pred[2048,2]{1,0:T(8,128)(4,1)S(1)} %copy-done.2, ...), kind=kLoop, calls=%fused_computation.2.clone.1 | loop fusion | flops 6815744 | bytes 10510337 | tf_op jit(solution)/shard_map/while/body/eval_jaxpr/add | solution.py:63
  434.0 17.5 %fusion.27 = (f32[2048,2,128]{2,1,0:T(2,128)}, f32[2048,2,128]{2,1,0:T(2,128)}) fusion(f32[2048,2,128]{2,1,0:T(2,128)} %get-tuple-element.256, pred[]{:T(512)S(6)} %compare.3, f32[2048,2,128]{2,1,0:T(2,128)} %get-tuple-element.255, f32[2048,128]{1,0:T(8,128)S(1)} %bitcast.93, pred[2048,2]{1,0:T(8,128)(4,1)S(1)} %copy-done.2, ...), kind=kLoop, calls=%fused_computation.2.clone.1 | loop fusion | flops 6815744 | bytes 10510337 | tf_op jit(solution)/shard_map/while/body/eval_jaxpr/add | solution.py:63
  464.5 17.5 %fusion.27 = (f32[2048,2,128]{2,1,0:T(2,128)}, f32[2048,2,128]{2,1,0:T(2,128)}) fusion(f32[2048,2,128]{2,1,0:T(2,128)} %get-tuple-element.256, pred[]{:T(512)S(6)} %compare.3, f32[2048,2,128]{2,1,0:T(2,128)} %get-tuple-element.255, f32[2048,128]{1,0:T(8,128)S(1)} %bitcast.93, pred[2048,2]{1,0:T(8,128)(4,1)S(1)} %copy-done.2, ...), kind=kLoop, calls=%fused_computation.2.clone.1 | loop fusion | flops 6815744 | bytes 10510337 | tf_op jit(solution)/shard_map/while/body/eval_jaxpr/add | solution.py:63
  495.0 17.5 %fusion.27 = (f32[2048,2,128]{2,1,0:T(2,128)}, f32[2048,2,128]{2,1,0:T(2,128)}) fusion(f32[2048,2,128]{2,1,0:T(2,128)} %get-tuple-element.256, pred[]{:T(512)S(6)} %compare.3, f32[2048,2,128]{2,1,0:T(2,128)} %get-tuple-element.255, f32[2048,128]{1,0:T(8,128)S(1)} %bitcast.93, pred[2048,2]{1,0:T(8,128)(4,1)S(1)} %copy-done.2, ...), kind=kLoop, calls=%fused_computation.2.clone.1 | loop fusion | flops 6815744 | bytes 10510337 | tf_op jit(solution)/shard_map/while/body/eval_jaxpr/add | solution.py:63
  525.5 17.5 %fusion.27 = (f32[2048,2,128]{2,1,0:T(2,128)}, f32[2048,2,128]{2,1,0:T(2,128)}) fusion(f32[2048,2,128]{2,1,0:T(2,128)} %get-tuple-element.256, pred[]{:T(512)S(6)} %compare.3, f32[2048,2,128]{2,1,0:T(2,128)} %get-tuple-element.255, f32[2048,128]{1,0:T(8,128)S(1)} %bitcast.93, pred[2048,2]{1,0:T(8,128)(4,1)S(1)} %copy-done.2, ...), kind=kLoop, calls=%fused_computation.2.clone.1 | loop fusion | flops 6815744 | bytes 10510337 | tf_op jit(solution)/shard_map/while/body/eval_jaxpr/add | solution.py:63
  556.0 17.5 %fusion.27 = (f32[2048,2,128]{2,1,0:T(2,128)}, f32[2048,2,128]{2,1,0:T(2,128)}) fusion(f32[2048,2,128]{2,1,0:T(2,128)} %get-tuple-element.256, pred[]{:T(512)S(6)} %compare.3, f32[2048,2,128]{2,1,0:T(2,128)} %get-tuple-element.255, f32[2048,128]{1,0:T(8,128)S(1)} %bitcast.93, pred[2048,2]{1,0:T(8,128)(4,1)S(1)} %copy-done.2, ...), kind=kLoop, calls=%fused_computation.2.clone.1 | loop fusion | flops 6815744 | bytes 10510337 | tf_op jit(solution)/shard_map/while/body/eval_jaxpr/add | solution.py:63
  586.5 17.5 %fusion.27 = (f32[2048,2,128]{2,1,0:T(2,128)}, f32[2048,2,128]{2,1,0:T(2,128)}) fusion(f32[2048,2,128]{2,1,0:T(2,128)} %get-tuple-element.256, pred[]{:T(512)S(6)} %compare.3, f32[2048,2,128]{2,1,0:T(2,128)} %get-tuple-element.255, f32[2048,128]{1,0:T(8,128)S(1)} %bitcast.93, pred[2048,2]{1,0:T(8,128)(4,1)S(1)} %copy-done.2, ...), kind=kLoop, calls=%fused_computation.2.clone.1 | loop fusion | flops 6815744 | bytes 10510337 | tf_op jit(solution)/shard_map/while/body/eval_jaxpr/add | solution.py:63
  607.4 41.1 %all_to_all.24 = bf16[2048,2,128]{2,1,0:T(2,128)(2,1)S(1)} all-to-all(bf16[2048,2,128]{2,1,0:T(2,128)(2,1)S(1)} %multiply_convert_fusion), channel_id=1, replica_groups=mesh['grp'=2,'skill'=16] {'skill'}, dimensions={0} | all-to-all | bytes 2097152 | tf_op jit(solution)/shard_map/all_to_all | solution.py:70
  (153 shorter events, 215.0 us)
Async XLA Ops:
  0.0 56.4 %copy-start = (bf16[1,16,4,128,128]{4,3,2,1,0:T(8,128)(2,1)S(1)}, bf16[1,16,4,128,128]{4,3,2,1,0:T(8,128)(2,1)}, u32[]{:S(2)}) copy-start(bf16[1,16,4,128,128]{4,3,2,1,0:T(8,128)(2,1)} %param.11) | copy-start | bytes 6291460
  14.6 33.8 %copy-start.6 = (f32[32,32]{1,0:T(8,128)S(1)}, f32[32,32]{1,0:T(8,128)}, u32[]{:S(2)}) copy-start(f32[32,32]{1,0:T(8,128)} %param.10) | copy-start | bytes 12292
  48.4 7.9 %copy-start.7 = (s32[1,16,4]{1,2,0:T(4,128)S(1)}, s32[1,16,4]{1,2,0:T(4,128)}, u32[]{:S(2)}) copy-start(s32[1,16,4]{1,2,0:T(4,128)} %param.12) | copy-start | bytes 772
  48.4 8.0 %copy-start.8 = (s32[1,16]{1,0:T(1,128)S(1)}, s32[1,16]{1,0:T(1,128)}, u32[]{:S(2)}) copy-start(s32[1,16]{1,0:T(1,128)} %param.13) | copy-start | bytes 196
  51.7 29.2 %collective-permute-start.2 = (bf16[2048,2,128]{2,1,0:T(2,128)(2,1)}, bf16[2048,2,128]{2,1,0:T(2,128)(2,1)S(1)}, u32[]{:S(2)}, u32[]{:S(2)}) collective-permute-start(bf16[2048,2,128]{2,1,0:T(2,128)(2,1)} %convert_element_type.25), channel_id=1, source_target_pairs={{3,0},{4,1},{5,2},{6,3},{7,4},{8,5},{9,6},{10,7},{11,8},{12,9},{13... | collective-permute-start | bytes 3145736 | tf_op jit(solution)/shard_map/ppermute | solution.py:10
  53.0 46.0 %collective-permute-start.1 = (bf16[2048,2,128]{2,1,0:T(2,128)(2,1)}, bf16[2048,2,128]{2,1,0:T(2,128)(2,1)}, u32[]{:S(2)}, u32[]{:S(2)}) collective-permute-start(bf16[2048,2,128]{2,1,0:T(2,128)(2,1)} %convert_element_type.25), channel_id=1, source_target_pairs={{2,0},{3,1},{4,2},{5,3},{6,4},{7,5},{8,6},{9,7},{10,8},{11,9},{12,... | collective-permute-start | bytes 3145736 | tf_op jit(solution)/shard_map/ppermute | solution.py:10
  54.3 46.5 %collective-permute-start = (bf16[2048,2,128]{2,1,0:T(2,128)(2,1)}, bf16[2048,2,128]{2,1,0:T(2,128)(2,1)}, u32[]{:S(2)}, u32[]{:S(2)}) collective-permute-start(bf16[2048,2,128]{2,1,0:T(2,128)(2,1)} %convert_element_type.25), channel_id=1, source_target_pairs={{1,0},{2,1},{3,2},{4,3},{5,4},{6,5},{7,6},{8,7},{9,8},{10,9},{11,1... | collective-permute-start | bytes 3145736 | tf_op jit(solution)/shard_map/ppermute | solution.py:10
  59.5 4.2 copy-start.4
  63.7 8.6 %copy-start.5 = (f32[16,2,2048]{2,1,0:T(2,128)S(1)}, f32[16,2,2048]{2,1,0:T(2,128)}, u32[]{:S(2)}) copy-start(f32[16,2,2048]{2,1,0:T(2,128)} %param.15) | copy-start | bytes 786436
  72.3 28.5 %copy-start.3 = (bf16[2048,2,128]{2,1,0:T(2,128)(2,1)S(1)}, bf16[2048,2,128]{2,1,0:T(2,128)(2,1)}, u32[]{:S(2)}) copy-start(bf16[2048,2,128]{2,1,0:T(2,128)(2,1)} %convert_element_type.25) | copy-start | bytes 3145732
  125.6 3.9 copy-start.2
  155.5 3.9 copy-start.2
  186.0 3.9 copy-start.2
  216.5 3.9 copy-start.2
  247.0 3.9 copy-start.2
  277.5 3.9 copy-start.2
  308.0 3.9 copy-start.2
  338.5 3.9 copy-start.2
  369.0 3.9 copy-start.2
  399.5 3.9 copy-start.2
  430.0 3.9 copy-start.2
  460.6 3.9 copy-start.2
  491.1 3.9 copy-start.2
  521.6 3.9 copy-start.2
  552.1 3.9 copy-start.2
  582.6 3.9 copy-start.2
  648.5 2.3 copy-start.1
